TPU v7x, 256 devices: a whole 4x4x8 slice. The times are simulated.
256 devices in a mesh: rows: 8 (over y, x_lo), cols: 32 (over z, x_hi, core).
Axes of the slice: x: 4 (x_hi: 2, x_lo: 2; x = x_hi * 2 + x_lo), y: 4, z: 8, core: 2. Of those that a mesh axis runs over, the one named last changes fastest.
Arguments:
- counts: bfloat16 [4096, 262144], P('rows', 'cols'), may hold values from 0 to 12, as said below
- start_a: float32 [4096, 128], P(('rows', 'cols')), may hold values from -0.4 to 0.4
- start_b: float32 [16384, 128], P(('cols', 'rows')), may hold values from -0.4 to 0.4
- start_c: float32 [16, 128], replicated, may hold values from -0.4 to 0.4
Outputs:
- factor_a: float32 [4096, 128], P(('rows', 'cols'))
- factor_b: float32 [16384, 128], P(('cols', 'rows'))
- factor_c: float32 [16, 128], replicated
Inputs may be any that keep to these rules, and one draw needn't show every extreme that they name: counts holds whole numbers.
All inputs are finite; a program needn't handle non-finite values.
Results may differ from a plain program's by a relative error of at most 0.009.
Values may be sent and summed in bfloat16 or wider, within the bound.
No kernel may reach another device: no remote copies, remote signals or barrier semaphores. Data moves between devices by JAX's collectives and lax.ppermute only.
A program may use at most 128 MiB of HBM per device.

v0:
```python
import math
import jax
import jax.numpy as jnp
from jax import lax
from jax.sharding import PartitionSpec as P

ITERS = 2


def local(counts, start_a, start_b, start_c):
    rows_here, flat_width = counts.shape
    depth = start_c.shape[0]
    cols_here = flat_width // depth
    total_i = rows_here * lax.axis_size("rows")
    total_j = cols_here * lax.axis_size("cols")
    rate_a = 0.3 / math.sqrt(total_j * depth)
    rate_b = 0.3 / math.sqrt(total_i * depth)
    rate_c = 0.3 / math.sqrt(total_i * total_j)
    local_a, local_b, shared_c = (start_a, start_b, start_c)
    for iteration in range(ITERS):
        low_a = lax.all_gather(local_a.astype(jnp.bfloat16), "cols", axis=0, tiled=True)
        low_b = lax.all_gather(local_b.astype(jnp.bfloat16), "rows", axis=0, tiled=True)
        low_b_wide = low_b.astype(jnp.float32)
        scaled = (low_b_wide[:, None, :] * shared_c[None, :, :]).astype(jnp.bfloat16)
        scaled = scaled.reshape(cols_here * depth, shared_c.shape[1])
        log_rate = lax.dot_general(
            low_a, scaled, (((1,), (1,)), ((), ())), preferred_element_type=jnp.float32
        )
        residual = (jnp.exp(log_rate) - counts.astype(jnp.float32)).astype(jnp.bfloat16)
        grad_a = jnp.dot(residual, scaled, preferred_element_type=jnp.float32)
        mixed = lax.dot_general(
            residual, low_a, (((0,), (0,)), ((), ())), preferred_element_type=jnp.float32
        )
        mixed = mixed.reshape(cols_here, depth, shared_c.shape[1])
        grad_b = jnp.sum(mixed * shared_c[None, :, :], axis=1)
        grad_c = jnp.sum(mixed * low_b_wide[:, None, :], axis=0)
        summed_a = lax.psum_scatter(grad_a, "cols", scatter_dimension=0, tiled=True)
        summed_b = lax.psum_scatter(grad_b, "rows", scatter_dimension=0, tiled=True)
        local_a = local_a - rate_a * summed_a
        local_b = local_b - rate_b * summed_b
        summed_c = lax.psum(grad_c, ("rows", "cols"))
        shared_c = shared_c - rate_c * summed_c
    return (local_a, local_b, shared_c)


def solution(mesh):
    placed = (P("rows", "cols"), P(("rows", "cols"), None), P(("cols", "rows"), None), P())
    return jax.shard_map(
        local,
        mesh=mesh,
        in_specs=placed,
        out_specs=(P(("rows", "cols"), None), P(("cols", "rows"), None), P()),
        check_vma=False,
    )
```

profile of v0, /device:TPU:32, one launch (start us, length us, event | category | flops | bytes accessed | tf_op | source)
XLA Modules:
  0.0 455.2 jit_solution(1326504930640590621)
XLA Ops:
  7.2 0.0 reduce-scatter.5.cloned.1.call-start
  7.2 12.0 %copy.7 = bf16[512,8192]{0,1:T(8,128)(2,1)} copy(bf16[512,8192]{1,0:T(8,128)(2,1)} %param.4) | data formatting | bytes 16777216 | tf_op args[0]
  19.2 28.6 %all_gather.12 = bf16[512,128]{1,0:T(8,128)(2,1)S(1)} all-gather(bf16[64,128]{1,0:T(8,128)(2,1)S(1)} %convert_element_type.42), channel_id=1, replica_groups=mesh['rows'=8,'cols'=32] {'rows'}, dimensions={0}, use_global_device_ids=true | all-gather | bytes 147456 | tf_op jit(solution)/shard_map/all_gather | solution.py:22
  47.9 42.5 %all_gather.13 = bf16[512,128]{1,0:T(8,128)(2,1)S(1)} all-gather(bf16[16,128]{1,0:T(8,128)(2,1)S(1)} %convert_element_type.46), channel_id=1, replica_groups=mesh['rows'=8,'cols'=32] {'cols'}, dimensions={0}, use_global_device_ids=true | all-gather | bytes 135168 | tf_op jit(solution)/shard_map/all_gather | solution.py:21
  90.4 0.4 multiply_convert_fusion.1
  90.8 5.0 %fusion = bf16[512,8192]{0,1:T(8,128)(2,1)S(1)} fusion(bf16[512,8192]{0,1:T(8,128)(2,1)} %copy.7, bf16[8192,128]{1,0:T(8,128)(2,1)S(1)} %bitcast.22, bf16[512,128]{1,0:T(8,128)(2,1)S(1)} %all_gather.13), kind=kOutput, calls=%fused_computation.2 | convolution fusion | flops 1086324736 | bytes 19005440 | tf_op jit(solution)/shard_map/dot_general | solution.py:26
  95.8 3.2 copy-done
  99.0 3.0 fusion.4
  102.1 0.0 reduce-scatter.7.cloned.1.call-start
  102.1 8.4 %multiply_reduce_fusion.3 = (f32[512,128]{1,0:T(8,128)}, f32[8192,128]{1,0:T(8,128)}) fusion(f32[16,128]{1,0:T(8,128)S(1)} %copy-done.5, bf16[512,8192]{0,1:T(8,128)(2,1)} %copy-done, bf16[512,128]{1,0:T(8,128)(2,1)S(1)} %all_gather.13), kind=kOutput, calls=%fused_computation.8 | convolution fusion | flops 1075773440 | bytes 12984320 | tf_op jit(solution)/shard_map/dot_general | solution.py:31
  110.5 0.0 reduce-scatter.9.cloned.1.call-start
  110.6 2.8 multiply_reduce_fusion.2
  113.4 77.1 %psum.14 = f32[16,128]{1,0:T(8,128)S(1)} all-reduce(f32[16,128]{1,0:T(8,128)S(1)} %multiply_reduce_fusion.2), channel_id=1, replica_groups=mesh['rows'=8,'cols'=32] {'rows','cols'}, use_global_device_ids=true, to_apply=%region_4.0 | all-reduce | flops 2048 | bytes 16384 | tf_op jit(solution)/shard_map/psum | solution.py:41
  190.5 21.8 %reduce-scatter.5.cloned.1.call-done = f32[16,128]{1,0:T(8,128)} async-done(((f32[512,128]{1,0:T(8,128)}), f32[16,128]{1,0:T(8,128)}) %reduce-scatter.5.cloned.1.call-update) | async-done | bytes 8208 | tf_op jit(solution)/shard_map/reduce_scatter | solution.py:37
  212.3 0.7 fusion.3
  213.0 38.0 %all_gather.14 = bf16[512,128]{1,0:T(8,128)(2,1)S(1)} all-gather(bf16[16,128]{1,0:T(8,128)(2,1)S(1)} %fusion.3), channel_id=1, replica_groups=mesh['rows'=8,'cols'=32] {'cols'}, dimensions={0}, use_global_device_ids=true | all-gather | bytes 135168 | tf_op jit(solution)/shard_map/all_gather | solution.py:21
  251.0 2.8 reduce-scatter.7.cloned.1.call-done
  253.8 0.8 fusion.2
  254.6 28.5 %all_gather.15 = bf16[512,128]{1,0:T(8,128)(2,1)S(1)} all-gather(bf16[64,128]{1,0:T(8,128)(2,1)S(1)} %fusion.2), channel_id=1, replica_groups=mesh['rows'=8,'cols'=32] {'rows'}, dimensions={0}, use_global_device_ids=true | all-gather | bytes 147456 | tf_op jit(solution)/shard_map/all_gather | solution.py:22
  283.1 0.4 multiply_convert_fusion
  283.5 5.0 %fusion.1 = bf16[512,8192]{0,1:T(8,128)(2,1)S(1)} fusion(bf16[512,8192]{0,1:T(8,128)(2,1)} %copy.7, bf16[512,128]{1,0:T(8,128)(2,1)S(1)} %all_gather.14, bf16[8192,128]{1,0:T(8,128)(2,1)S(1)} %bitcast.24), kind=kOutput, calls=%fused_computation.3 | convolution fusion | flops 1086324736 | bytes 19005440 | tf_op jit(solution)/shard_map/dot_general | solution.py:26
  288.5 3.2 copy-done.1
  291.7 3.1 fusion.5
  294.8 0.0 reduce-scatter.11.cloned.1.call-start
  294.9 8.4 %multiply_reduce_fusion.1 = (f32[512,128]{1,0:T(8,128)}, f32[8192,128]{1,0:T(8,128)}) fusion(f32[16,128]{1,0:T(8,128)S(1)} %multiply_subtract_fusion.4, bf16[512,8192]{0,1:T(8,128)(2,1)} %copy-done.1, bf16[512,128]{1,0:T(8,128)(2,1)S(1)} %all_gather.14), kind=kOutput, calls=%fused_computation.5 | convolution fusion | flops 1075773440 | bytes 12984320 | tf_op jit(solution)/shard_map/dot_general | solution.py:31
  303.3 2.8 multiply_reduce_fusion
  306.1 73.2 %psum.15 = f32[16,128]{1,0:T(8,128)S(1)} all-reduce(f32[16,128]{1,0:T(8,128)S(1)} %multiply_reduce_fusion), channel_id=1, replica_groups=mesh['rows'=8,'cols'=32] {'rows','cols'}, use_global_device_ids=true, to_apply=%region_9.0 | all-reduce | flops 2048 | bytes 16384 | tf_op jit(solution)/shard_map/psum | solution.py:41
  379.4 0.6 multiply_subtract_fusion.2
  380.0 25.9 %reduce-scatter.9.cloned.1.call-done = f32[16,128]{1,0:T(8,128)} async-done(((f32[512,128]{1,0:T(8,128)}), f32[16,128]{1,0:T(8,128)}) %reduce-scatter.9.cloned.1.call-update) | async-done | bytes 8208 | tf_op jit(solution)/shard_map/reduce_scatter | solution.py:37
  405.9 1.3 multiply_subtract_fusion.3
  407.2 40.1 %reduce-scatter.11.cloned.1.call-done = f32[64,128]{1,0:T(8,128)} async-done(((f32[512,128]{1,0:T(8,128)}), f32[64,128]{1,0:T(8,128)}) %reduce-scatter.11.cloned.1.call-update) | async-done | bytes 32784 | tf_op jit(solution)/shard_map/reduce_scatter | solution.py:38
  447.3 1.4 multiply_subtract_fusion
  (21 shorter events, 0.1 us)
Async XLA Ops:
  7.2 12.0 %copy-start.2 = (f32[64,128]{1,0:T(8,128)S(1)}, f32[64,128]{1,0:T(8,128)}, u32[]{:S(2)}) copy-start(f32[64,128]{1,0:T(8,128)} %param.6) | copy-start | bytes 98308
  7.2 40.7 %copy-start.4 = (f32[16,128]{1,0:T(8,128)S(1)}, f32[16,128]{1,0:T(8,128)}, u32[]{:S(2)}) copy-start(f32[16,128]{1,0:T(8,128)} %param.5) | copy-start | bytes 24580
  7.2 83.2 %copy-start.5 = (f32[16,128]{1,0:T(8,128)S(1)}, f32[16,128]{1,0:T(8,128)}, u32[]{:S(2)}) copy-start(f32[16,128]{1,0:T(8,128)} %param.7) | copy-start | bytes 24580
  7.2 205.1 %reduce-scatter.5.cloned.1.call-start = ((), (), s32[]{:S(2)}) async-start(), calls=%async_computation.4 | async-start | bytes 270336 | tf_op jit(solution)/shard_map/reduce_scatter | solution.py:37
  95.8 3.2 copy-start
  102.1 151.7 %reduce-scatter.7.cloned.1.call-start = ((), (), s32[]{:S(2)}) async-start(), calls=%async_computation.5 | async-start | bytes 294912 | tf_op jit(solution)/shard_map/reduce_scatter | solution.py:38
  110.5 295.3 %reduce-scatter.9.cloned.1.call-start = ((), (), s32[]{:S(2)}) async-start(), calls=%async_computation.6 | async-start | bytes 270336 | tf_op jit(solution)/shard_map/reduce_scatter | solution.py:37
  288.5 3.2 copy-start.1
  294.8 152.5 %reduce-scatter.11.cloned.1.call-start = ((), (), s32[]{:S(2)}) async-start(), calls=%async_computation.7 | async-start | bytes 294912 | tf_op jit(solution)/shard_map/reduce_scatter | solution.py:38
  303.3 102.6 %copy-start.6 = (f32[16,128]{1,0:T(8,128)S(1)}, f32[16,128]{1,0:T(8,128)}, u32[]{:S(2)}) copy-start(f32[16,128]{1,0:T(8,128)} %reduce-scatter.5.cloned.1.call-done) | copy-start | bytes 24580
  303.3 144.0 %copy-start.3 = (f32[64,128]{1,0:T(8,128)S(1)}, f32[64,128]{1,0:T(8,128)}, u32[]{:S(2)}) copy-start(f32[64,128]{1,0:T(8,128)} %reduce-scatter.7.cloned.1.call-done) | copy-start | bytes 98308
Sparse Core Ops, SparseCore 0:
  102.2 110.0 reduce-scatter.4
  214.8 38.9 reduce-scatter.6
  294.9 110.8 reduce-scatter.8
  408.4 38.8 reduce-scatter.10
where the time goes:
time: 456 us; the launch traced here: 455 us
  blocking collectives  288 us (63%)
  waiting for transfers between devices  90.7 us (20%)
  matrix products  33 us (7%)
  local copies, waits for them, and re-layouts  18.4 us (4%)
  between operations  13.9 us (3%)
  other arithmetic  11.1 us (2%)
    psum x2, blocking collectives, local(): summed_c = lax.psum(grad_c, ('rows', 'cols'))  150 us
    all_gather x2, blocking collectives, local(): lax.all_gather(local_a.astype(jnp.bfloat16), 'cols', axis=0, tiled=True)  80.5 us
    all_gather x2, blocking collectives, local(): lax.all_gather(local_b.astype(jnp.bfloat16), 'rows', axis=0, tiled=True)  57.1 us
    reduce_scatter x2, waiting for transfers between devices, local(): summed_a = lax.psum_scatter(grad_a, 'cols', scatter_dimension=0, tiled=True)  47.7 us
    reduce_scatter x2, waiting for transfers between devices, local(): summed_b = lax.psum_scatter(grad_b, 'rows', scatter_dimension=0, tiled=True)  42.9 us
    unnamed x15, local copies, waits for them, and re-layouts  18.4 us
    dot_general x2, matrix products, local(): lax.dot_general(residual, low_a, (((0,), (0,)), ((), ())), preferred_elem...  16.8 us
    dot_general x2, matrix products, local(): lax.dot_general(low_a, scaled, (((1,), (1,)), ((), ())), preferred_elemen...  10.1 us
  transfers between devices with their start and end apart: 4, of which 4 were waited for; matrix products, arithmetic and copies ran while one was open for 5% of the time, Pallas kernels for 0%

commit v1 on v0

--- a/solution.py
+++ b/solution.py
@@ -38,7 +38,9 @@
         summed_b = lax.psum_scatter(grad_b, "rows", scatter_dimension=0, tiled=True)
         local_a = local_a - rate_a * summed_a
         local_b = local_b - rate_b * summed_b
-        summed_c = lax.psum(grad_c, ("rows", "cols"))
+        summed_c = grad_c
+        for axis in ("rows", "cols"):
+            summed_c = lax.psum(summed_c, axis)
         shared_c = shared_c - rate_c * summed_c
     return (local_a, local_b, shared_c)
 

time: 456 us -> 456 us (level)
  blocking collectives: 288 us -> 293 us
  waiting for transfers between devices: 90.7 us -> 85.7 us
    reduce_scatter x2, waiting for transfers between devices: 47.7 us -> 42.8 us  [local(): summed_a = lax.psum_scatter(grad_a, 'cols', scatter_dimension=0, tiled=True)]
    psum x2 -> x4, blocking collectives: 150 us -> 155 us  [local(): summed_c = lax.psum(summed_c, axis)]
where the time goes in v1:
time: 456 us; the launch traced here: 455 us
  blocking collectives  293 us (64%)
  waiting for transfers between devices  85.7 us (19%)
  matrix products  33 us (7%)
  local copies, waits for them, and re-layouts  18.4 us (4%)
  between operations  13.9 us (3%)
  other arithmetic  11.1 us (2%)
    psum x4, blocking collectives, local(): summed_c = lax.psum(summed_c, axis)  155 us
    all_gather x2, blocking collectives, local(): lax.all_gather(local_a.astype(jnp.bfloat16), 'cols', axis=0, tiled=True)  80.6 us
    all_gather x2, blocking collectives, local(): lax.all_gather(local_b.astype(jnp.bfloat16), 'rows', axis=0, tiled=True)  57.1 us
    reduce_scatter x2, waiting for transfers between devices, local(): summed_a = lax.psum_scatter(grad_a, 'cols', scatter_dimension=0, tiled=True)  42.8 us
    reduce_scatter x2, waiting for transfers between devices, local(): summed_b = lax.psum_scatter(grad_b, 'rows', scatter_dimension=0, tiled=True)  42.8 us
    unnamed x15, local copies, waits for them, and re-layouts  18.4 us
    dot_general x2, matrix products, local(): lax.dot_general(residual, low_a, (((0,), (0,)), ((), ())), preferred_elem...  16.8 us
    dot_general x2, matrix products, local(): lax.dot_general(low_a, scaled, (((1,), (1,)), ((), ())), preferred_elemen...  10.1 us
  transfers between devices with their start and end apart: 4, of which 4 were waited for; matrix products, arithmetic and copies ran while one was open for 5% of the time, Pallas kernels for 0%

profile of v1, /device:TPU:32, one launch (start us, length us, event | category | flops | bytes accessed | tf_op | source)
XLA Modules:
  0.0 455.2 jit_solution(10490463855169546024)
XLA Ops:
  7.2 12.0 %copy.7 = bf16[512,8192]{0,1:T(8,128)(2,1)} copy(bf16[512,8192]{1,0:T(8,128)(2,1)} %param.4) | data formatting | bytes 16777216 | tf_op args[0]
  19.2 28.6 %all_gather.12 = bf16[512,128]{1,0:T(8,128)(2,1)S(1)} all-gather(bf16[64,128]{1,0:T(8,128)(2,1)S(1)} %convert_element_type.42), channel_id=1, replica_groups=mesh['rows'=8,'cols'=32] {'rows'}, dimensions={0}, use_global_device_ids=true | all-gather | bytes 147456 | tf_op jit(solution)/shard_map/all_gather | solution.py:22
  47.9 42.5 %all_gather.13 = bf16[512,128]{1,0:T(8,128)(2,1)S(1)} all-gather(bf16[16,128]{1,0:T(8,128)(2,1)S(1)} %convert_element_type.46), channel_id=1, replica_groups=mesh['rows'=8,'cols'=32] {'cols'}, dimensions={0}, use_global_device_ids=true | all-gather | bytes 135168 | tf_op jit(solution)/shard_map/all_gather | solution.py:21
  90.4 0.4 multiply_convert_fusion.1
  90.8 5.0 %fusion = bf16[512,8192]{0,1:T(8,128)(2,1)S(1)} fusion(bf16[512,8192]{0,1:T(8,128)(2,1)} %copy.7, bf16[8192,128]{1,0:T(8,128)(2,1)S(1)} %bitcast.22, bf16[512,128]{1,0:T(8,128)(2,1)S(1)} %all_gather.13), kind=kOutput, calls=%fused_computation.2 | convolution fusion | flops 1086324736 | bytes 19005440 | tf_op jit(solution)/shard_map/dot_general | solution.py:26
  95.8 3.2 copy-done
  99.0 3.0 fusion.4
  102.1 0.0 reduce-scatter.7.cloned.1.call-start
  102.1 8.4 %multiply_reduce_fusion.3 = (f32[512,128]{1,0:T(8,128)}, f32[8192,128]{1,0:T(8,128)}) fusion(f32[16,128]{1,0:T(8,128)S(1)} %copy-done.5, bf16[512,8192]{0,1:T(8,128)(2,1)} %copy-done, bf16[512,128]{1,0:T(8,128)(2,1)S(1)} %all_gather.13), kind=kOutput, calls=%fused_computation.8 | convolution fusion | flops 1075773440 | bytes 12984320 | tf_op jit(solution)/shard_map/dot_general | solution.py:31
  110.5 0.0 reduce-scatter.9.cloned.1.call-start
  110.6 2.8 multiply_reduce_fusion.2
  113.4 19.1 %psum.28 = f32[16,128]{1,0:T(8,128)S(1)} all-reduce(f32[16,128]{1,0:T(8,128)S(1)} %multiply_reduce_fusion.2), channel_id=1, replica_groups=mesh['rows'=8,'cols'=32] {'rows'}, use_global_device_ids=true, to_apply=%region_4.0 | all-reduce | flops 2048 | bytes 16384 | tf_op jit(solution)/shard_map/psum | solution.py:43
  132.4 59.9 %psum.29 = f32[16,128]{1,0:T(8,128)S(1)} all-reduce(f32[16,128]{1,0:T(8,128)S(1)} %psum.28), channel_id=1, replica_groups=mesh['rows'=8,'cols'=32] {'cols'}, use_global_device_ids=true, to_apply=%region_5.0 | all-reduce | flops 2048 | bytes 16384 | tf_op jit(solution)/shard_map/psum | solution.py:43
  192.3 20.0 %reduce-scatter.5.cloned.1.call-done = f32[16,128]{1,0:T(8,128)} async-done(((f32[512,128]{1,0:T(8,128)}), f32[16,128]{1,0:T(8,128)}) %reduce-scatter.5.cloned.1.call-update) | async-done | bytes 8208 | tf_op jit(solution)/shard_map/reduce_scatter | solution.py:37
  212.4 0.7 fusion.3
  213.1 38.1 %all_gather.14 = bf16[512,128]{1,0:T(8,128)(2,1)S(1)} all-gather(bf16[16,128]{1,0:T(8,128)(2,1)S(1)} %fusion.3), channel_id=1, replica_groups=mesh['rows'=8,'cols'=32] {'cols'}, dimensions={0}, use_global_device_ids=true | all-gather | bytes 135168 | tf_op jit(solution)/shard_map/all_gather | solution.py:21
  251.2 2.7 reduce-scatter.7.cloned.1.call-done
  253.9 0.8 fusion.2
  254.7 28.5 %all_gather.15 = bf16[512,128]{1,0:T(8,128)(2,1)S(1)} all-gather(bf16[64,128]{1,0:T(8,128)(2,1)S(1)} %fusion.2), channel_id=1, replica_groups=mesh['rows'=8,'cols'=32] {'rows'}, dimensions={0}, use_global_device_ids=true | all-gather | bytes 147456 | tf_op jit(solution)/shard_map/all_gather | solution.py:22
  283.2 0.4 multiply_convert_fusion
  283.5 5.0 %fusion.1 = bf16[512,8192]{0,1:T(8,128)(2,1)S(1)} fusion(bf16[512,8192]{0,1:T(8,128)(2,1)} %copy.7, bf16[512,128]{1,0:T(8,128)(2,1)S(1)} %all_gather.14, bf16[8192,128]{1,0:T(8,128)(2,1)S(1)} %bitcast.24), kind=kOutput, calls=%fused_computation.3 | convolution fusion | flops 1086324736 | bytes 19005440 | tf_op jit(solution)/shard_map/dot_general | solution.py:26
  288.6 3.2 copy-done.1
  291.8 3.1 fusion.5
  294.9 8.4 %multiply_reduce_fusion.1 = (f32[512,128]{1,0:T(8,128)}, f32[8192,128]{1,0:T(8,128)}) fusion(f32[16,128]{1,0:T(8,128)S(1)} %multiply_subtract_fusion.4, bf16[512,8192]{0,1:T(8,128)(2,1)} %copy-done.1, bf16[512,128]{1,0:T(8,128)(2,1)S(1)} %all_gather.14), kind=kOutput, calls=%fused_computation.5 | convolution fusion | flops 1075773440 | bytes 12984320 | tf_op jit(solution)/shard_map/dot_general | solution.py:31
  303.4 2.8 multiply_reduce_fusion
  306.2 16.8 %psum.30 = f32[16,128]{1,0:T(8,128)S(1)} all-reduce(f32[16,128]{1,0:T(8,128)S(1)} %multiply_reduce_fusion), channel_id=1, replica_groups=mesh['rows'=8,'cols'=32] {'rows'}, use_global_device_ids=true, to_apply=%region_10.0 | all-reduce | flops 2048 | bytes 16384 | tf_op jit(solution)/shard_map/psum | solution.py:43
  322.9 59.6 %psum.31 = f32[16,128]{1,0:T(8,128)S(1)} all-reduce(f32[16,128]{1,0:T(8,128)S(1)} %psum.30), channel_id=1, replica_groups=mesh['rows'=8,'cols'=32] {'cols'}, use_global_device_ids=true, to_apply=%region_11.0 | all-reduce | flops 2048 | bytes 16384 | tf_op jit(solution)/shard_map/psum | solution.py:43
  382.5 0.6 multiply_subtract_fusion.2
  383.1 22.8 %reduce-scatter.9.cloned.1.call-done = f32[16,128]{1,0:T(8,128)} async-done(((f32[512,128]{1,0:T(8,128)}), f32[16,128]{1,0:T(8,128)}) %reduce-scatter.9.cloned.1.call-update) | async-done | bytes 8208 | tf_op jit(solution)/shard_map/reduce_scatter | solution.py:37
  405.9 1.3 multiply_subtract_fusion.3
  407.2 40.1 %reduce-scatter.11.cloned.1.call-done = f32[64,128]{1,0:T(8,128)} async-done(((f32[512,128]{1,0:T(8,128)}), f32[64,128]{1,0:T(8,128)}) %reduce-scatter.11.cloned.1.call-update) | async-done | bytes 32784 | tf_op jit(solution)/shard_map/reduce_scatter | solution.py:38
  447.3 1.4 multiply_subtract_fusion
  (23 shorter events, 0.2 us)
Async XLA Ops:
  7.2 12.0 %copy-start.2 = (f32[64,128]{1,0:T(8,128)S(1)}, f32[64,128]{1,0:T(8,128)}, u32[]{:S(2)}) copy-start(f32[64,128]{1,0:T(8,128)} %param.6) | copy-start | bytes 98308
  7.2 40.7 %copy-start.4 = (f32[16,128]{1,0:T(8,128)S(1)}, f32[16,128]{1,0:T(8,128)}, u32[]{:S(2)}) copy-start(f32[16,128]{1,0:T(8,128)} %param.5) | copy-start | bytes 24580
  7.2 83.2 %copy-start.5 = (f32[16,128]{1,0:T(8,128)S(1)}, f32[16,128]{1,0:T(8,128)}, u32[]{:S(2)}) copy-start(f32[16,128]{1,0:T(8,128)} %param.7) | copy-start | bytes 24580
  7.2 205.2 %reduce-scatter.5.cloned.1.call-start = ((), (), s32[]{:S(2)}) async-start(), calls=%async_computation.4 | async-start | bytes 270336 | tf_op jit(solution)/shard_map/reduce_scatter | solution.py:37
  95.8 3.2 copy-start
  102.1 151.8 %reduce-scatter.7.cloned.1.call-start = ((), (), s32[]{:S(2)}) async-start(), calls=%async_computation.5 | async-start | bytes 294912 | tf_op jit(solution)/shard_map/reduce_scatter | solution.py:38
  110.5 295.4 %reduce-scatter.9.cloned.1.call-start = ((), (), s32[]{:S(2)}) async-start(), calls=%async_computation.6 | async-start | bytes 270336 | tf_op jit(solution)/shard_map/reduce_scatter | solution.py:37
  288.6 3.2 copy-start.1
  294.9 152.4 %reduce-scatter.11.cloned.1.call-start = ((), (), s32[]{:S(2)}) async-start(), calls=%async_computation.7 | async-start | bytes 294912 | tf_op jit(solution)/shard_map/reduce_scatter | solution.py:38
  303.4 102.5 %copy-start.6 = (f32[16,128]{1,0:T(8,128)S(1)}, f32[16,128]{1,0:T(8,128)}, u32[]{:S(2)}) copy-start(f32[16,128]{1,0:T(8,128)} %reduce-scatter.5.cloned.1.call-done) | copy-start | bytes 24580
  303.4 143.9 %copy-start.3 = (f32[64,128]{1,0:T(8,128)S(1)}, f32[64,128]{1,0:T(8,128)}, u32[]{:S(2)}) copy-start(f32[64,128]{1,0:T(8,128)} %reduce-scatter.7.cloned.1.call-done) | copy-start | bytes 98308
Sparse Core Ops, SparseCore 0:
  102.2 110.0 reduce-scatter.4
  214.9 38.9 reduce-scatter.6
  295.0 110.8 reduce-scatter.8
  408.4 38.8 reduce-scatter.10
